TPU v7x, 256 devices: a whole 4x4x8 slice. The times are simulated.
256 devices in a mesh: row: 8 (over z), col: 16 (over x_hi, y, core), pan: 2 (over x_lo).
Axes of the slice: x: 4 (x_hi: 2, x_lo: 2; x = x_hi * 2 + x_lo), y: 4, z: 8, core: 2. Of those that a mesh axis runs over, the one named last changes fastest.
Arguments:
- gradient: bfloat16 [8192, 28672], P('row', ('col', 'pan')), may hold values from -240 to 240
- stat_old: float32 [8192, 1024], P(('row', 'col', 'pan')), may hold values from -4800 to 4800, as said below
Outputs:
- preconditioned: float32 [8192, 28672], P('row', ('col', 'pan'))
- stat_new: float32 [8192, 1024], P(('row', 'col', 'pan'))
Inputs may be any that keep to these rules, and one draw needn't show every extreme that they name: Each block of 1024 rows of stat_old is a symmetric positive definite matrix.
All inputs are finite; a program needn't handle non-finite values.
Results may differ from a plain program's by a relative error of at most 0.0003.
Values sent between devices are 32-bit elements; how exact they have to be, the bound alone decides.
No kernel may reach another device: no remote copies, remote signals or barrier semaphores. Data moves between devices by JAX's collectives and lax.ppermute only.
A program may use at most 64 MiB of HBM per device.

v0:
```python
import jax
import jax.numpy as jnp
from jax import lax
from jax.sharding import PartitionSpec as P

COLS = 28672
damping = 0.001
stat_decay = 0.9
newton_scale = 2.5


def local(gradient, stat_old):
    highest = lax.Precision.HIGHEST
    panel_rows = stat_old.shape[0]
    order_size = stat_old.shape[1]
    offset = lax.axis_index(("col", "pan")) * panel_rows
    weight_new = (1.0 - stat_decay) / COLS
    row_ids = lax.broadcasted_iota(jnp.int32, (panel_rows, order_size), 0) + offset
    col_ids = lax.broadcasted_iota(jnp.int32, (panel_rows, order_size), 1)
    eye_panel = (row_ids == col_ids).astype(jnp.float32)
    eye_whole = jnp.eye(order_size, dtype=jnp.float32)
    contract = (((1,), (1,)), ((), ()))
    partial_value = lax.dot_general(
        gradient, gradient, contract, preferred_element_type=jnp.float32
    )
    placed = lax.dynamic_update_slice_in_dim(
        jnp.zeros((order_size, order_size), jnp.float32), stat_decay * stat_old, offset, 0
    )
    stat_whole = lax.psum(weight_new * partial_value + placed, ("col", "pan"))
    stat_new = lax.dynamic_slice_in_dim(stat_whole, offset, panel_rows, 0)
    matrix = stat_whole + damping * eye_whole
    frobenius = jnp.sqrt(jnp.sum(matrix * matrix))
    scaled = newton_scale * matrix / frobenius
    first_step = 1.25 * eye_whole - 0.25 * scaled
    square = jnp.dot(first_step, first_step, precision=highest)
    square_panel = lax.dynamic_slice_in_dim(square, offset, panel_rows, 0)
    fourth_panel = jnp.dot(square_panel, square, precision=highest)
    moved_panel = jnp.dot(fourth_panel, scaled, precision=highest)
    second_panel = 1.25 * eye_panel - 0.25 * moved_panel
    product = jnp.dot(second_panel, first_step, precision=highest)
    root_panel = (frobenius / newton_scale) ** (-0.25) * product
    preconditioned = jnp.dot(
        lax.all_gather(root_panel, ("col", "pan"), axis=0, tiled=True),
        gradient,
        precision=highest,
        preferred_element_type=jnp.float32,
    )
    return (preconditioned, stat_new)


def solution(mesh):
    placed = (P("row", ("col", "pan")), P(("row", "col", "pan"), None))
    return jax.shard_map(
        local,
        mesh=mesh,
        in_specs=placed,
        out_specs=(P("row", ("col", "pan")), P(("row", "col", "pan"), None)),
        check_vma=False,
    )
```

profile of v0, /device:TPU:1, one launch (start us, length us, event | category | flops | bytes accessed | tf_op | source)
XLA Modules:
  0.0 281.0 jit_solution(15637310542160839473)
XLA Ops:
  7.2 0.0 copy-start
  7.2 0.0 all-reduce.2.cloned.1.call-start
  7.2 1.4 copy-done
  8.7 0.0 copy-start.2
  8.7 4.3 %convolution_multiply_fusion = f32[1024,1024]{1,0:T(8,128)} fusion(bf16[1024,896]{1,0:T(8,128)(2,1)S(1)} %copy-done), kind=kOutput, calls=%fused_computation.7 | convolution fusion | flops 1880096768 | bytes 6029312 | tf_op jit(solution)/shard_map/dot_general | solution.py:23
  13.0 0.0 copy-done.2
  13.0 1.6 add_dynamic-update-slice_fusion
  14.6 0.0 all-reduce.2.cloned.1.call-update
  14.6 0.0 all-gather.2.cloned.1.call-start
  14.7 125.5 %all-reduce.2.cloned.1.call-done = f32[1024,1024]{1,0:T(8,128)} async-done(((f32[1024,1024]{1,0:T(8,128)}), f32[1024,1024]{1,0:T(8,128)}) %all-reduce.2.cloned.1.call-update) | async-done | bytes 4194320 | tf_op jit(solution)/shard_map/psum | solution.py:29
  140.2 3.9 %multiply_reduce_fusion = f32[]{:T(128)} fusion(f32[1024,1024]{1,0:T(8,128)} %all-reduce.2.cloned.1.call-done), kind=kLoop, calls=%fused_computation.2 | loop fusion | flops 5242879 | bytes 4194308 | tf_op jit(solution)/shard_map/reduce_sum | solution.py:32
  144.8 19.9 %fusion.1 = f32[1024,1024]{1,0:T(8,128)S(1)} fusion(f32[1024,1024]{1,0:T(8,128)} %all-reduce.2.cloned.1.call-done, f32[]{:T(128)S(6)} %sqrt.3), kind=kOutput, calls=%fused_computation.6 | convolution fusion | flops 12893290496 | bytes 8388612 | tf_op jit(solution)/shard_map/dot_general | solution.py:35
  164.7 2.5 fusion.10
  167.2 0.0 copy-start.1
  167.2 5.1 %fusion.8 = f32[32,1024]{1,0:T(8,128)S(1)} fusion(f32[32,1024]{1,0:T(8,128)S(1)} %fusion.10, s32[32]{0:T(128)S(1)} %iota_add_fusion, f32[1024,1024]{1,0:T(8,128)} %all-reduce.2.cloned.1.call-done, f32[]{:T(128)S(6)} %sqrt.3), kind=kOutput, calls=%fused_computation.15 | convolution fusion | flops 408027136 | bytes 4456580 | tf_op jit(solution)/shard_map/dot_general | solution.py:38
  172.4 0.0 copy-done.1
  172.4 3.7 %fusion.9 = f32[32,1024]{1,0:T(8,128)} fusion(f32[32,1024]{1,0:T(8,128)S(1)} %fusion.8, f32[]{:T(128)S(6)} %pow.3, f32[1024,1024]{1,0:T(8,128)S(1)} %copy-done.1, f32[]{:T(128)S(6)} %sqrt.3), kind=kOutput, calls=%fused_computation.16 | convolution fusion | flops 411074560 | bytes 4456456 | tf_op jit(solution)/shard_map/dot_general | solution.py:40
  176.1 0.0 all-gather.2.cloned.1.call-update
  176.1 1.6 constant_dynamic-slice_fusion
  177.7 86.8 %all-gather.2.cloned.1.call-done = f32[1024,1024]{1,0:T(8,128)} async-done(((f32[32,1024]{1,0:T(8,128)}), f32[1024,1024]{1,0:T(8,128)}) %all-gather.2.cloned.1.call-update) | async-done | bytes 4194320 | tf_op jit(solution)/shard_map/all_gather | solution.py:43
  264.5 9.6 %fusion.19 = f32[1024,896]{1,0:T(8,128)} fusion(f32[1024,1024]{1,0:T(8,128)} %all-gather.2.cloned.1.call-done, bf16[1024,896]{1,0:T(8,128)(2,1)S(1)} %copy-done), kind=kOutput, calls=%fused_computation.30 | convolution fusion | flops 11274289152 | bytes 9699328 | tf_op jit(solution)/shard_map/dot_general | solution.py:42
  (1 shorter events, 0.0 us)
Async XLA Ops:
  7.2 1.5 copy-start
  7.2 133.0 %all-reduce.2.cloned.1.call-start = ((), (), s32[]{:S(2)}) async-start(), calls=%async_computation | async-start | bytes 8388608 | tf_op jit(solution)/shard_map/psum | solution.py:29
  8.7 4.3 %copy-start.2 = (f32[32,1024]{1,0:T(8,128)S(1)}, f32[32,1024]{1,0:T(8,128)}, u32[]{:S(2)}) copy-start(f32[32,1024]{1,0:T(8,128)} %param.3) | copy-start | bytes 393220
  14.6 249.9 %all-gather.2.cloned.1.call-start = ((), (), s32[]{:S(2)}) async-start(), calls=%async_computation.1 | async-start | bytes 4325376 | tf_op jit(solution)/shard_map/all_gather | solution.py:43
  167.2 5.1 %copy-start.1 = (f32[1024,1024]{1,0:T(8,128)S(1)}, f32[1024,1024]{1,0:T(8,128)}, u32[]{:S(2)}) copy-start(f32[1024,1024]{1,0:T(8,128)} %all-reduce.2.cloned.1.call-done) | copy-start | bytes 12582916
Sparse Core Ops, SparseCore 0:
  14.7 125.4 all-reduce.1
  176.3 88.1 all-gather.1
where the time goes:
time: 281 us
  waiting for transfers between devices  212 us (75%)
  matrix products  45.2 us (16%)
  between operations  14.9 us (5%)
  other arithmetic  5.45 us (2%)
  local copies, waits for them, and re-layouts  3.03 us (1%)
    psum x1, waiting for transfers between devices, local(): stat_whole = lax.psum(weight_new * partial_value + placed, ('col', 'pan'))  126 us
    all_gather x1, waiting for transfers between devices, local(): lax.all_gather(root_panel, ('col', 'pan'), axis=0, tiled=True)  86.8 us
    dot_general x1, matrix products, local(): square = jnp.dot(first_step, first_step, precision=highest)  19.9 us
    dot_general x1, matrix products, local(): jnp.dot(lax.all_gather(root_panel, ('col', 'pan'), axis=0, tiled=True), g...  9.65 us
  transfers between devices with their start and end apart: 2, of which 2 were waited for; matrix products, arithmetic and copies ran while one was open for 1% of the time, Pallas kernels for 0%

commit v1 on v0

--- a/solution.py
+++ b/solution.py
@@ -40,7 +40,15 @@
     product = jnp.dot(second_panel, first_step, precision=highest)
     root_panel = (frobenius / newton_scale) ** (-0.25) * product
     preconditioned = jnp.dot(
-        lax.all_gather(root_panel, ("col", "pan"), axis=0, tiled=True),
+        jnp.concatenate(
+            lax.all_to_all(
+                jnp.stack([root_panel] * lax.axis_size(("col", "pan")), 0),
+                axis_name=("col", "pan"),
+                split_axis=0,
+                concat_axis=0,
+            ),
+            0,
+        ),
         gradient,
         precision=highest,
         preferred_element_type=jnp.float32,

time: 281 us -> 255 us (0.907); the launches traced: 281 us -> 251 us
  waiting for transfers between devices: 212 us -> 175 us
  starting transfers between devices: 0.08 us -> 5.99 us
    all_gather x1 -> x0, waiting for transfers between devices: 86.8 us -> none  [local(): lax.all_gather(root_panel, ('col', 'pan'), axis=0, tiled=True)]
    all_to_all x0 -> x1, waiting for transfers between devices: none -> 49.3 us  [local(): lax.all_to_all(jnp.stack([root_panel] * lax.axis_size(('col', 'pan')), 0)...]
    all_to_all x0 -> x1, starting transfers between devices: none -> 5.95 us  [local(): lax.all_to_all(jnp.stack([root_panel] * lax.axis_size(('col', 'pan')), 0)...]
where the time goes in v1:
time: 255 us; the launch traced here: 251 us
  waiting for transfers between devices  175 us (69%)
  matrix products  44.6 us (17%)
  between operations  14.9 us (6%)
  starting transfers between devices  5.99 us (2%)
  local copies, waits for them, and re-layouts  5.51 us (2%)
  other arithmetic  5.46 us (2%)
    psum x1, waiting for transfers between devices, local(): stat_whole = lax.psum(weight_new * partial_value + placed, ('col', 'pan'))  126 us
    all_to_all x1, waiting for transfers between devices, local(): lax.all_to_all(jnp.stack([root_panel] * lax.axis_size(('col', 'pan')), 0)...  49.3 us
    dot_general x1, matrix products, local(): square = jnp.dot(first_step, first_step, precision=highest)  19.9 us
    dot_general x1, matrix products, local(): jnp.dot(jnp.concatenate(lax.all_to_all(jnp.stack([root_panel] * lax.axis_...  9.65 us
    all_to_all x1, starting transfers between devices, local(): lax.all_to_all(jnp.stack([root_panel] * lax.axis_size(('col', 'pan')), 0)...  5.95 us
    dot_general x1, matrix products, local(): moved_panel = jnp.dot(fourth_panel, scaled, precision=highest)  5.12 us
  transfers between devices with their start and end apart: 2, of which 2 were waited for; matrix products, arithmetic and copies ran while one was open for 1% of the time, Pallas kernels for 0%

profile of v1, /device:TPU:1, one launch (start us, length us, event | category | flops | bytes accessed | tf_op | source)
XLA Modules:
  0.0 251.3 jit_solution(7673776842577927502)
XLA Ops:
  7.2 0.0 copy-start
  7.2 0.0 all-reduce.2.cloned.1.call-start
  7.2 1.4 copy-done
  8.7 0.0 copy-start.2
  8.7 4.3 %convolution_multiply_fusion = f32[1024,1024]{1,0:T(8,128)} fusion(bf16[1024,896]{1,0:T(8,128)(2,1)S(1)} %copy-done), kind=kOutput, calls=%fused_computation.7 | convolution fusion | flops 1880096768 | bytes 6029312 | tf_op jit(solution)/shard_map/dot_general | solution.py:23
  13.0 0.0 copy-done.2
  13.0 1.6 add_dynamic-update-slice_fusion
  14.6 0.0 all-reduce.2.cloned.1.call-update
  14.6 125.7 %all-reduce.2.cloned.1.call-done = f32[1024,1024]{1,0:T(8,128)} async-done(((f32[1024,1024]{1,0:T(8,128)}), f32[1024,1024]{1,0:T(8,128)}) %all-reduce.2.cloned.1.call-update) | async-done | bytes 4194320 | tf_op jit(solution)/shard_map/psum | solution.py:29
  140.3 3.9 %multiply_reduce_fusion = f32[]{:T(128)} fusion(f32[1024,1024]{1,0:T(8,128)} %all-reduce.2.cloned.1.call-done), kind=kLoop, calls=%fused_computation.2 | loop fusion | flops 5242879 | bytes 4194308 | tf_op jit(solution)/shard_map/reduce_sum | solution.py:32
  144.9 19.9 %fusion.1 = f32[1024,1024]{1,0:T(8,128)S(1)} fusion(f32[1024,1024]{1,0:T(8,128)} %all-reduce.2.cloned.1.call-done, f32[]{:T(128)S(6)} %sqrt.3), kind=kOutput, calls=%fused_computation.6 | convolution fusion | flops 12893290496 | bytes 8388612 | tf_op jit(solution)/shard_map/dot_general | solution.py:35
  164.8 2.5 fusion.10
  167.3 0.0 copy-start.1
  167.3 5.1 %fusion.8 = f32[32,1024]{1,0:T(8,128)S(1)} fusion(f32[32,1024]{1,0:T(8,128)S(1)} %fusion.10, s32[32]{0:T(128)S(1)} %iota_add_fusion, f32[1024,1024]{1,0:T(8,128)} %all-reduce.2.cloned.1.call-done, f32[]{:T(128)S(6)} %sqrt.3), kind=kOutput, calls=%fused_computation.15 | convolution fusion | flops 408027136 | bytes 4456580 | tf_op jit(solution)/shard_map/dot_general | solution.py:38
  172.5 0.0 copy-done.1
  172.5 3.1 %fusion.9 = f32[32,1024]{1,0:T(8,128)S(1)} fusion(f32[32,1024]{1,0:T(8,128)S(1)} %fusion.8, f32[]{:T(128)S(6)} %pow.3, f32[1024,1024]{1,0:T(8,128)S(1)} %copy-done.1, f32[]{:T(128)S(6)} %sqrt.3), kind=kOutput, calls=%fused_computation.16 | convolution fusion | flops 411074560 | bytes 4456456 | tf_op jit(solution)/shard_map/dot_general | solution.py:40
  175.5 2.5 stack.2
  178.0 6.0 %all-to-all-start = ((f32[32,32,1024]{2,1,0:T(8,128)}), f32[32,32,1024]{2,1,0:T(8,128)}, u32[]{:S(2)}, u32[]{:S(2)}) async-start(f32[32,32,1024]{2,1,0:T(8,128)} %stack.2), calls=%async_computation | async-start | bytes 8388608 | tf_op jit(solution)/shard_map/all_to_all | solution.py:44
  184.0 1.6 constant_dynamic-slice_fusion
  185.6 49.3 %all-to-all-done = f32[32,32,1024]{2,1,0:T(8,128)} async-done(((f32[32,32,1024]{2,1,0:T(8,128)}), f32[32,32,1024]{2,1,0:T(8,128)}, u32[]{:S(2)}, u32[]{:S(2)}) %all-to-all-start) | async-done | bytes 4194336 | tf_op jit(solution)/shard_map/all_to_all | solution.py:44
  234.8 9.6 %fusion.19 = f32[1024,896]{1,0:T(8,128)} fusion(f32[1024,1024]{1,0:T(8,128)} %bitcast, bf16[1024,896]{1,0:T(8,128)(2,1)S(1)} %copy-done), kind=kOutput, calls=%fused_computation.30 | convolution fusion | flops 11274289152 | bytes 9699328 | tf_op jit(solution)/shard_map/dot_general | solution.py:42
  (1 shorter events, 0.0 us)
Async XLA Ops:
  7.2 1.5 copy-start
  7.2 133.1 %all-reduce.2.cloned.1.call-start = ((), (), s32[]{:S(2)}) async-start(), calls=%async_computation.1 | async-start | bytes 8388608 | tf_op jit(solution)/shard_map/psum | solution.py:29
  8.7 4.3 %copy-start.2 = (f32[32,1024]{1,0:T(8,128)S(1)}, f32[32,1024]{1,0:T(8,128)}, u32[]{:S(2)}) copy-start(f32[32,1024]{1,0:T(8,128)} %param.3) | copy-start | bytes 393220
  167.3 5.1 %copy-start.1 = (f32[1024,1024]{1,0:T(8,128)S(1)}, f32[1024,1024]{1,0:T(8,128)}, u32[]{:S(2)}) copy-start(f32[1024,1024]{1,0:T(8,128)} %all-reduce.2.cloned.1.call-done) | copy-start | bytes 12582916
  178.0 56.8 %all-to-all-start = ((f32[32,32,1024]{2,1,0:T(8,128)}), f32[32,32,1024]{2,1,0:T(8,128)}, u32[]{:S(2)}, u32[]{:S(2)}) async-start(f32[32,32,1024]{2,1,0:T(8,128)} %stack.2), calls=%async_computation | async-start | bytes 8388608 | tf_op jit(solution)/shard_map/all_to_all | solution.py:44
Sparse Core Ops, SparseCore 0:
  14.7 125.5 all-reduce.1
